TPU v7x, 32 devices: a whole 2x2x4 slice. The times are simulated.
32 devices in a mesh: dp: 2 (over y), seq: 16 (over z, x, core).
Axes of the slice: x: 2, y: 2, z: 4, core: 2. Of those that a mesh axis runs over, the one named last changes fastest.
Arguments:
- layer_input: bfloat16 [2, 2048, 1024], P('dp', 'seq'), may hold values from -12 to 12
- v_first: bfloat16 [2, 2048, 1024], P('dp', 'seq'), may hold values from -6 to 6
- cotangent: bfloat16 [2, 2048, 1024], P('dp', 'seq'), may hold values from -6 to 6
- segments: int32 [2, 2048], P('dp'), may hold values from 0 to 3, never falling along the last dimension, each value on 1 to 1024 neighbouring positions
- norm1_gain: bfloat16 [1024], P('seq'), may hold values from 0.099609375 to 1.8984375
- w_query: bfloat16 [1024, 1024], P('seq', 'dp'), may hold values from -0.1875 to 0.1875
- w_key: bfloat16 [1024, 1024], P('seq', 'dp'), may hold values from -0.1875 to 0.1875
- w_value: bfloat16 [1024, 1024], P('seq', 'dp'), may hold values from -0.1875 to 0.1875
- w_out: bfloat16 [1024, 1024], P('seq', 'dp'), may hold values from -1.5 to 1.5
- norm2_gain: bfloat16 [1024], P('seq'), may hold values from 0.099609375 to 1.8984375
- w_gate: bfloat16 [1024, 2816], P('seq', 'dp'), may hold values from -0.1875 to 0.1875
- w_up: bfloat16 [1024, 2816], P('seq', 'dp'), may hold values from -0.1875 to 0.1875
- w_down: bfloat16 [2816, 1024], P('seq', 'dp'), may hold values from -0.109375 to 0.109375
Outputs:
- out: bfloat16 [2, 2048, 1024], P('dp', 'seq')
- d_input: bfloat16 [2, 2048, 1024], P('dp', 'seq')
- d_v_first: bfloat16 [2, 2048, 1024], P('dp', 'seq')
- d_norm1_gain: float32 [1024], P('seq')
- d_w_query: float32 [1024, 1024], P('seq', 'dp')
- d_w_key: float32 [1024, 1024], P('seq', 'dp')
- d_w_value: float32 [1024, 1024], P('seq', 'dp')
- d_w_out: float32 [1024, 1024], P('seq', 'dp')
- d_norm2_gain: float32 [1024], P('seq')
- d_w_gate: float32 [1024, 2816], P('seq', 'dp')
- d_w_up: float32 [1024, 2816], P('seq', 'dp')
- d_w_down: float32 [2816, 1024], P('seq', 'dp')
- rms: float32 [3], replicated
Inputs may be any that keep to these rules, and one draw needn't show every extreme that they name: `segments`: in each row the ids start at 0 and never fall; every id up to 3 is used, by at most 1024 tokens.
All inputs are finite; a program needn't handle non-finite values.
Results may differ from a plain program's by a relative error of at most 0.022.
Values may be sent and summed in bfloat16 or wider, within the bound.
No kernel may reach another device: no remote copies, remote signals or barrier semaphores. Data moves between devices by JAX's collectives and lax.ppermute only.
A program may use at most 256 MiB of HBM per device.

v0:
```python
import jax
import jax.numpy as jnp
from jax import lax
from jax.sharding import PartitionSpec as P

H = 16
HS = 64
EPSILON = 1e-06


def normalize(rows_in, gain_in):
    return (
        rows_in * lax.rsqrt(jnp.mean(rows_in * rows_in, axis=-1, keepdims=True) + EPSILON) * gain_in
    )


def rotary_tables(positions):
    half_size = HS // 2
    frequency = 10000.0 ** (-jnp.arange(half_size, dtype=jnp.float32) * 2.0 / HS)
    angles = positions[..., None] * frequency
    return (jnp.cos(angles)[..., None, :], jnp.sin(angles)[..., None, :])


def rotate(values, cosine, sine_t):
    shaped = values.reshape(values.shape[:-1] + (H, HS))
    half_size = HS // 2
    lower_half = shaped[..., :half_size]
    upper_half = shaped[..., half_size:]
    turned = jnp.concatenate(
        [lower_half * cosine - upper_half * sine_t, upper_half * cosine + lower_half * sine_t],
        axis=-1,
    )
    return turned.reshape(values.shape)


def project(rows_in, weight):
    return jnp.einsum("sqi,ij->sqj", rows_in, weight, preferred_element_type=jnp.float32)


def project_back(grad_rows, weight):
    return jnp.einsum("sqj,ij->sqi", grad_rows, weight, preferred_element_type=jnp.float32)


def weight_grad(left_rows, right_rows):
    return jnp.einsum("sqi,sqj->ij", left_rows, right_rows, preferred_element_type=jnp.float32)


def fetch_forward(w_query, w_key, w_value, w_out, w_gate, w_up, w_down, norm1_gain, norm2_gain):
    wide_set = (
        lax.all_gather(w_query, "dp", axis=1, tiled=True),
        lax.all_gather(w_key, "dp", axis=1, tiled=True),
        lax.all_gather(w_value, "dp", axis=1, tiled=True),
        lax.all_gather(w_out, "dp", axis=1, tiled=True),
        lax.all_gather(w_gate, "dp", axis=1, tiled=True),
        lax.all_gather(w_up, "dp", axis=1, tiled=True),
        lax.all_gather(w_down, "dp", axis=1, tiled=True),
    )
    return (
        lax.all_gather(wide_set[0], "seq", axis=0, tiled=True),
        lax.all_gather(wide_set[1], "seq", axis=0, tiled=True),
        lax.all_gather(wide_set[2], "seq", axis=0, tiled=True),
        lax.all_gather(wide_set[3], "seq", axis=0, tiled=True),
        lax.all_gather(wide_set[4], "seq", axis=0, tiled=True),
        lax.all_gather(wide_set[5], "seq", axis=0, tiled=True),
        lax.all_gather(wide_set[6], "seq", axis=0, tiled=True),
        lax.all_gather(norm1_gain, "seq", axis=0, tiled=True),
        lax.all_gather(norm2_gain, "seq", axis=0, tiled=True),
    )


def fetch_backward(w_query, w_key, w_value, w_out, w_gate, w_up, w_down, norm1_gain, norm2_gain):
    wide_set = (
        lax.all_gather(w_query, "dp", axis=1, tiled=True),
        lax.all_gather(w_key, "dp", axis=1, tiled=True),
        lax.all_gather(w_value, "dp", axis=1, tiled=True),
        lax.all_gather(w_out, "dp", axis=1, tiled=True),
        lax.all_gather(w_gate, "dp", axis=1, tiled=True),
        lax.all_gather(w_up, "dp", axis=1, tiled=True),
        lax.all_gather(w_down, "dp", axis=1, tiled=True),
    )
    return (
        lax.all_gather(wide_set[0], "seq", axis=0, tiled=True),
        lax.all_gather(wide_set[1], "seq", axis=0, tiled=True),
        lax.all_gather(wide_set[2], "seq", axis=0, tiled=True),
        lax.all_gather(wide_set[3], "seq", axis=0, tiled=True),
        lax.all_gather(wide_set[4], "seq", axis=0, tiled=True),
        lax.all_gather(wide_set[5], "seq", axis=0, tiled=True),
        lax.all_gather(wide_set[6], "seq", axis=0, tiled=True),
        lax.all_gather(norm1_gain, "seq", axis=0, tiled=True),
        lax.all_gather(norm2_gain, "seq", axis=0, tiled=True),
    )


def local(
    layer_input,
    v_first,
    cotangent,
    segments,
    norm1_gain,
    w_query,
    w_key,
    w_value,
    w_out,
    norm2_gain,
    w_gate,
    w_up,
    w_down,
):
    num_seqs, own_tokens, model_width = layer_input.shape
    length = segments.shape[1]
    block_rows = min(1024, length)
    block_count = length // block_rows
    score_scale = HS ** (-0.5)
    offset = lax.axis_index("seq") * own_tokens
    own_seg = lax.dynamic_slice_in_dim(segments, offset, own_tokens, 1)
    own_index = offset + jnp.arange(own_tokens, dtype=jnp.int32)
    starts = jnp.sum((segments[:, None, :] < own_seg[:, :, None]).astype(jnp.int32), axis=2)
    cosine, sine_t = rotary_tables((own_index[None, :] - starts).astype(jnp.float32))
    block_ids = jnp.arange(block_count)
    full_set = fetch_forward(
        w_query, w_key, w_value, w_out, w_gate, w_up, w_down, norm1_gain, norm2_gain
    )
    input_f = layer_input.astype(jnp.float32)
    gain_one = full_set[7].astype(jnp.float32)
    gain_two = full_set[8].astype(jnp.float32)
    normed_one = normalize(input_f, gain_one).astype(jnp.bfloat16)
    query_raw = project(normed_one, full_set[0])
    key_raw = project(normed_one, full_set[1])
    mixed_values = (
        0.5 * project(normed_one, full_set[2]) + 0.5 * v_first.astype(jnp.float32)
    ).astype(jnp.bfloat16)
    q_rot = rotate(query_raw, cosine, sine_t).astype(jnp.bfloat16)
    k_rot = rotate(key_raw, cosine, sine_t).astype(jnp.bfloat16)
    keys_all, values_all = (
        lax.all_gather(k_rot, "seq", axis=1, tiled=True),
        lax.all_gather(mixed_values, "seq", axis=1, tiled=True),
    )
    keys_h = keys_all.reshape(num_seqs, length, H, HS)
    values_h = values_all.reshape(num_seqs, length, H, HS)
    query_h = q_rot.reshape(num_seqs, own_tokens, H, HS)

    def masked_scores(block_no):
        first_row = block_no * block_rows
        key_block = lax.dynamic_slice_in_dim(keys_h, first_row, block_rows, 1)
        value_block = lax.dynamic_slice_in_dim(values_h, first_row, block_rows, 1)
        seg_block = lax.dynamic_slice_in_dim(segments, first_row, block_rows, 1)
        key_index = first_row + jnp.arange(block_rows, dtype=jnp.int32)
        raw_scores = (
            jnp.einsum("sqhd,skhd->shqk", query_h, key_block, preferred_element_type=jnp.float32)
            * score_scale
        )
        allowed = (seg_block[:, None, :] == own_seg[:, :, None]) & (
            key_index[None, None, :] <= own_index[None, :, None]
        )
        return (jnp.where(allowed[:, None], raw_scores, -1e30), key_block, value_block)

    def lse_step(carried, block_no):
        running_max, running_sum = carried
        scores, _, _ = masked_scores(block_no)
        new_max = jnp.maximum(running_max, jnp.max(scores, axis=-1))
        running_sum = running_sum * jnp.exp(running_max - new_max) + jnp.sum(
            jnp.exp(scores - new_max[..., None]), axis=-1
        )
        return ((new_max, running_sum), None)

    stat_shape = (num_seqs, H, own_tokens)
    (running_max, running_sum), _ = lax.scan(
        lse_step,
        (jnp.full(stat_shape, -1e30, jnp.float32), jnp.zeros(stat_shape, jnp.float32)),
        block_ids,
    )
    log_total = running_max + jnp.log(running_sum)

    def attend_step(carried, block_no):
        scores, _, value_block = masked_scores(block_no)
        soft_b = jnp.exp(scores - log_total[..., None]).astype(jnp.bfloat16)
        return (
            carried
            + jnp.einsum(
                "shqk,skhd->sqhd", soft_b, value_block, preferred_element_type=jnp.float32
            ),
            None,
        )

    head_zeros = jnp.zeros((num_seqs, own_tokens, H, HS), jnp.float32)
    attended_f, _ = lax.scan(attend_step, head_zeros, block_ids)
    attended = attended_f.reshape(num_seqs, own_tokens, H * HS).astype(jnp.bfloat16)
    branch_a = project(attended, full_set[3])
    hidden_in = input_f + branch_a
    normed_two = normalize(hidden_in, gain_two).astype(jnp.bfloat16)
    gate_pre = project(normed_two, full_set[4])
    upward = project(normed_two, full_set[5])
    activated = (jax.nn.silu(gate_pre) * upward).astype(jnp.bfloat16)
    branch_m = project(activated, full_set[6])
    result = hidden_in + branch_m
    squares = jnp.stack(
        [jnp.sum(result * result), jnp.sum(branch_a * branch_a), jnp.sum(branch_m * branch_m)]
    )
    reused = fetch_backward(
        w_query, w_key, w_value, w_out, w_gate, w_up, w_down, norm1_gain, norm2_gain
    )
    grad_down = weight_grad(activated, cotangent)
    d_activated = project_back(cotangent, reused[6])
    gate_pull = jax.vjp(lambda gate_in, up_in: jax.nn.silu(gate_in) * up_in, gate_pre, upward)[1]
    d_gate_f, d_upward_f = gate_pull(d_activated)
    d_gate = d_gate_f.astype(jnp.bfloat16)
    d_upward = d_upward_f.astype(jnp.bfloat16)
    grad_gate = weight_grad(normed_two, d_gate)
    grad_up = weight_grad(normed_two, d_upward)
    d_normed_two = project_back(d_gate, reused[4]) + project_back(d_upward, reused[5])
    norm_pull_two = jax.vjp(normalize, hidden_in, gain_two)[1]
    d_hidden_part, d_gain_two = norm_pull_two(d_normed_two)
    d_hidden = cotangent.astype(jnp.float32) + d_hidden_part
    d_branch_a = d_hidden.astype(jnp.bfloat16)
    grad_out = weight_grad(attended, d_branch_a)
    d_attended = project_back(d_branch_a, reused[3]).astype(jnp.bfloat16)
    grad_h = d_attended.reshape(num_seqs, own_tokens, H, HS)

    def delta_step(carried, block_no):
        scores, _, value_block = masked_scores(block_no)
        soft_weights = jnp.exp(scores - log_total[..., None])
        d_soft = jnp.einsum(
            "sqhd,skhd->shqk", grad_h, value_block, preferred_element_type=jnp.float32
        )
        return (carried + jnp.sum(soft_weights * d_soft, axis=-1), None)

    row_delta, _ = lax.scan(delta_step, jnp.zeros(stat_shape, jnp.float32), block_ids)

    def score_grads(block_no):
        scores, key_block, value_block = masked_scores(block_no)
        soft_weights = jnp.exp(scores - log_total[..., None])
        d_soft = jnp.einsum(
            "sqhd,skhd->shqk", grad_h, value_block, preferred_element_type=jnp.float32
        )
        d_scores = (soft_weights * (d_soft - row_delta[..., None])).astype(jnp.bfloat16)
        return (soft_weights.astype(jnp.bfloat16), d_scores, key_block)

    def query_and_key(carried, block_no):
        soft_b, d_scores, key_block = score_grads(block_no)
        carried = carried + jnp.einsum(
            "shqk,skhd->sqhd", d_scores, key_block, preferred_element_type=jnp.float32
        )
        d_key_part = (
            jnp.einsum("shqk,sqhd->skhd", d_scores, query_h, preferred_element_type=jnp.float32)
            * score_scale
        )
        d_value_part = jnp.einsum(
            "shqk,sqhd->skhd", soft_b, grad_h, preferred_element_type=jnp.float32
        )
        return (carried, (d_key_part, d_value_part))

    d_query_h, (key_parts, value_parts) = lax.scan(query_and_key, head_zeros, block_ids)
    key_terms = jnp.moveaxis(key_parts, 0, 1).reshape(num_seqs, length, H * HS)
    value_terms = jnp.moveaxis(value_parts, 0, 1).reshape(num_seqs, length, H * HS)
    d_key_own, d_value_own = (
        lax.psum_scatter(
            key_terms.astype(jnp.bfloat16), "seq", scatter_dimension=1, tiled=True
        ).astype(jnp.float32),
        lax.psum_scatter(
            value_terms.astype(jnp.bfloat16), "seq", scatter_dimension=1, tiled=True
        ).astype(jnp.float32),
    )
    d_query_rot = d_query_h.reshape(num_seqs, own_tokens, H * HS) * score_scale
    d_query = rotate(d_query_rot, cosine, -sine_t).astype(jnp.bfloat16)
    d_key = rotate(d_key_own, cosine, -sine_t).astype(jnp.bfloat16)
    d_value = (0.5 * d_value_own).astype(jnp.bfloat16)
    grad_query = weight_grad(normed_one, d_query)
    grad_key = weight_grad(normed_one, d_key)
    grad_value = weight_grad(normed_one, d_value)
    d_normed_one = (
        project_back(d_query, reused[0])
        + project_back(d_key, reused[1])
        + project_back(d_value, reused[2])
    )
    norm_pull_one = jax.vjp(normalize, input_f, gain_one)[1]
    d_input_part, d_gain_one = norm_pull_one(d_normed_one)
    d_input = (d_hidden + d_input_part).astype(jnp.bfloat16)
    owned = (
        lax.psum_scatter(
            grad_query.astype(jnp.bfloat16), "seq", scatter_dimension=0, tiled=True
        ).astype(jnp.float32),
        lax.psum_scatter(
            grad_key.astype(jnp.bfloat16), "seq", scatter_dimension=0, tiled=True
        ).astype(jnp.float32),
        lax.psum_scatter(
            grad_value.astype(jnp.bfloat16), "seq", scatter_dimension=0, tiled=True
        ).astype(jnp.float32),
        lax.psum_scatter(
            grad_out.astype(jnp.bfloat16), "seq", scatter_dimension=0, tiled=True
        ).astype(jnp.float32),
        lax.psum_scatter(
            grad_gate.astype(jnp.bfloat16), "seq", scatter_dimension=0, tiled=True
        ).astype(jnp.float32),
        lax.psum_scatter(
            grad_up.astype(jnp.bfloat16), "seq", scatter_dimension=0, tiled=True
        ).astype(jnp.float32),
        lax.psum_scatter(
            grad_down.astype(jnp.bfloat16), "seq", scatter_dimension=0, tiled=True
        ).astype(jnp.float32),
    )
    final_set = (
        lax.psum_scatter(
            owned[0].astype(jnp.bfloat16), "dp", scatter_dimension=1, tiled=True
        ).astype(jnp.float32),
        lax.psum_scatter(
            owned[1].astype(jnp.bfloat16), "dp", scatter_dimension=1, tiled=True
        ).astype(jnp.float32),
        lax.psum_scatter(
            owned[2].astype(jnp.bfloat16), "dp", scatter_dimension=1, tiled=True
        ).astype(jnp.float32),
        lax.psum_scatter(
            owned[3].astype(jnp.bfloat16), "dp", scatter_dimension=1, tiled=True
        ).astype(jnp.float32),
        lax.psum_scatter(
            owned[4].astype(jnp.bfloat16), "dp", scatter_dimension=1, tiled=True
        ).astype(jnp.float32),
        lax.psum_scatter(
            owned[5].astype(jnp.bfloat16), "dp", scatter_dimension=1, tiled=True
        ).astype(jnp.float32),
        lax.psum_scatter(
            owned[6].astype(jnp.bfloat16), "dp", scatter_dimension=1, tiled=True
        ).astype(jnp.float32),
    )
    square_sums, gain_sums = lax.psum((squares, jnp.stack([d_gain_one, d_gain_two])), ("dp", "seq"))
    cell_count = num_seqs * own_tokens * model_width * lax.axis_size("dp") * lax.axis_size("seq")
    root_mean = jnp.sqrt(square_sums / cell_count)
    share = model_width // lax.axis_size("seq")
    gain_grads = lax.dynamic_slice_in_dim(gain_sums, lax.axis_index("seq") * share, share, 1)
    return (
        result.astype(jnp.bfloat16),
        d_input,
        d_value,
        gain_grads[0],
        final_set[0],
        final_set[1],
        final_set[2],
        final_set[3],
        gain_grads[1],
        final_set[4],
        final_set[5],
        final_set[6],
        root_mean,
    )


def solution(mesh):
    in_specs = (
        P("dp", "seq", None),
        P("dp", "seq", None),
        P("dp", "seq", None),
        P("dp", None),
        P("seq"),
        P("seq", "dp"),
        P("seq", "dp"),
        P("seq", "dp"),
        P("seq", "dp"),
        P("seq"),
        P("seq", "dp"),
        P("seq", "dp"),
        P("seq", "dp"),
    )
    out_specs = (
        P("dp", "seq", None),
        P("dp", "seq", None),
        P("dp", "seq", None),
        P("seq"),
        P("seq", "dp"),
        P("seq", "dp"),
        P("seq", "dp"),
        P("seq", "dp"),
        P("seq"),
        P("seq", "dp"),
        P("seq", "dp"),
        P("seq", "dp"),
        P(),
    )
    return jax.shard_map(local, mesh=mesh, in_specs=in_specs, out_specs=out_specs, check_vma=False)
```

profile of v0, /device:TPU:0, one launch (start us, length us, event | category | flops | bytes accessed | tf_op | source)
XLA Modules:
  0.0 1275.8 jit_solution(10179041738339998207)
XLA Ops:
  30.1 31.1 %all-reduce.3 = (bf16[1024]{0:T(1024)(128)(2,1)S(1)}, bf16[1024]{0:T(1024)(128)(2,1)S(1)}) all-reduce(bf16[1024]{0:T(1024)(128)(2,1)S(1)} %dynamic-update-slice, bf16[1024]{0:T(1024)(128)(2,1)S(1)} %dynamic-update-slice.1), channel_id=1, replica_groups=mesh['dp'=2,'seq'=16] {'seq'}, use_global_device_ids=true, to_apply=%add | all-reduce | flops 2048 | bytes 8192
  66.4 33.0 %all-gather.14.cloned.1.call-done = bf16[1024,1024]{1,0:T(8,128)(2,1)} async-done(((bf16[64,1024]{1,0:T(8,128)(2,1)}), bf16[1024,1024]{1,0:T(8,128)(2,1)}) %all-gather.14.cloned.1.call-update) | async-done | bytes 2097168 | tf_op jit(solution)/shard_map/all_gather | solution.py:60
  102.3 39.5 %all-gather.18.cloned.1.call-done = bf16[1024,1024]{1,0:T(8,128)(2,1)} async-done(((bf16[64,1024]{1,0:T(8,128)(2,1)}), bf16[1024,1024]{1,0:T(8,128)(2,1)}) %all-gather.18.cloned.1.call-update) | async-done | bytes 2097168 | tf_op jit(solution)/shard_map/all_gather | solution.py:59
  174.5 19.0 %all-gather.12.cloned.1.call-done = bf16[1,2048,1024]{2,1,0:T(8,128)(2,1)} async-done(((bf16[1,128,1024]{2,1,0:T(8,128)(2,1)}), bf16[1,2048,1024]{2,1,0:T(8,128)(2,1)}) %all-gather.12.cloned.1.call-update) | async-done | bytes 4194320 | tf_op jit(solution)/shard_map/all_gather | solution.py:136
  200.0 47.1 %all-gather.16.cloned.1.call-done = bf16[1,2048,1024]{1,2,0:T(8,128)(2,1)} async-done(((bf16[1,128,1024]{1,2,0:T(8,128)(2,1)}), bf16[1,2048,1024]{1,2,0:T(8,128)(2,1)}) %all-gather.16.cloned.1.call-update) | async-done | bytes 4194320 | tf_op jit(solution)/shard_map/all_gather | solution.py:135
  247.1 13.8 %while.50 = (s32[]{:T(128)}, f32[1,16,128]{2,1,0:T(8,128)S(1)}, f32[1,16,128]{2,1,0:T(8,128)S(1)}, s32[2]{0:T(128)S(1)}, s32[1,2048]{1,0:T(1,128)S(1)}, /*index=...) while((s32[]{:T(128)}, f32[1,16,128]{2,1,0:T(8,128)S(1)}, ...), condition=%wide.region_5.6_spmd.clone, body=%wide.region_2.5_spmd.clone.sunk | while | flops 283520128 | bytes 19658456 | solution.py:167
  260.9 14.2 %while.51 = (s32[]{:T(128)}, f32[1,128,16,64]{1,3,2,0:T(8,128)S(1)}, s32[2]{0:T(128)S(1)}, bf16[1,2048,16,64]{1,3,2,0:T(8,128)(2,1)}, s32[1,2048]{1,0:T(1,128)S(...) while((s32[]{:T(128)}, ...), condition=%wide.region_7.8_spmd.clone, body=%wide.region_6.7_spmd.clone.sunk | while | flops 545916032 | bytes 5799132 | solution.py:186
  275.2 13.6 %all-gather.20.cloned.1.call-done = bf16[1024,1024]{1,0:T(8,128)(2,1)} async-done(((bf16[64,1024]{1,0:T(8,128)(2,1)}), bf16[1024,1024]{1,0:T(8,128)(2,1)}) %all-gather.20.cloned.1.call-update) | async-done | bytes 2097168 | tf_op jit(solution)/shard_map/all_gather | solution.py:62
  291.8 56.7 %all-gather.24.cloned.1.call-done = bf16[1024,2816]{1,0:T(8,128)(2,1)} async-done(((bf16[64,2816]{1,0:T(8,128)(2,1)}), bf16[1024,2816]{1,0:T(8,128)(2,1)}) %all-gather.24.cloned.1.call-update) | async-done | bytes 5767184 | tf_op jit(solution)/shard_map/all_gather | solution.py:64
  353.1 55.0 %all-gather.22.cloned.1.call-done = bf16[1024,2816]{1,0:T(8,128)(2,1)} async-done(((bf16[64,2816]{1,0:T(8,128)(2,1)}), bf16[1024,2816]{1,0:T(8,128)(2,1)}) %all-gather.22.cloned.1.call-update) | async-done | bytes 5767184 | tf_op jit(solution)/shard_map/all_gather | solution.py:63
  412.8 54.9 %all-gather.26.cloned.1.call-done = bf16[2816,1024]{1,0:T(8,128)(2,1)} async-done(((bf16[176,1024]{1,0:T(8,128)(2,1)}), bf16[2816,1024]{1,0:T(8,128)(2,1)}) %all-gather.26.cloned.1.call-update) | async-done | bytes 5767184 | tf_op jit(solution)/shard_map/all_gather | solution.py:65
  489.5 17.2 %while.52 = (s32[]{:T(128)}, f32[1,16,128]{2,1,0:T(8,128)}, s32[2]{0:T(128)S(1)}, s32[1,2048]{1,0:T(1,128)S(1)}, s32[1,128]{1,0:T(1,128)S(1)}, /*index=5*/bf16[1...) while((s32[]{:T(128)}, f32[1,16,128]{2,1,0:T(8,128)}, ...), condition=%wide.region_12.13_spmd.clone, body=%wide.region_10.12_spmd.clone.sunk | while | flops 547753088 | bytes 38696792 | solution.py:227
  506.8 36.4 %while.53 = (s32[]{:T(128)}, f32[1,128,16,64]{1,3,2,0:T(8,128)S(1)}, bf16[2,1,1024,16,64]{2,4,3,1,0:T(8,128)(2,1)}, bf16[2,1,1024,16,64]{2,4,3,1,0:T(8,128)(2,1)...) while((s32[]{:T(128)}, ...), condition=%wide.region_14.15_spmd.clone, body=%wide.region_13.14_spmd.clone.sunk | while | flops 1364853888 | bytes 122140600 | solution.py:252
  543.2 11.0 copy.77
  554.2 11.9 reshape.1041
  566.1 11.0 copy.84
  577.1 28.8 %reshape.1048 = bf16[1,2048,1024]{2,0,1:T(2,128)(2,1)} reshape(bf16[2,1,1024,16,64]{4,3,2,0,1:T(8,128)(2,1)} %copy.84) | data formatting | bytes 8388608
  627.8 15.2 %reduce-scatter.23.cloned.1.call-done = bf16[1,128,1024]{2,1,0:T(8,128)(2,1)} async-done(((bf16[1,2048,1024]{2,1,0:T(8,128)(2,1)}), bf16[1,128,1024]{2,1,0:T(8,128)(2,1)}) %reduce-scatter.23.cloned.1.call-update) | async-done | bytes 262160 | tf_op jit(solution)/shard_map/reduce_scatter | solution.py:259
  646.3 72.3 %reduce-scatter.49.cloned.1.call-done = bf16[128,1024]{1,0:T(8,128)(2,1)} async-done(((bf16[2048,1024]{1,0:T(8,128)(2,1)}), bf16[128,1024]{1,0:T(8,128)(2,1)}) %reduce-scatter.49.cloned.1.call-update) | async-done | bytes 262160
  725.1 77.9 %reduce-scatter.43.cloned.1.call-done = bf16[64,2816]{1,0:T(8,128)(2,1)} async-done(((bf16[1024,2816]{1,0:T(8,128)(2,1)}), bf16[64,2816]{1,0:T(8,128)(2,1)}) %reduce-scatter.43.cloned.1.call-update) | async-done | bytes 360464 | tf_op jit(solution)/shard_map/reduce_scatter | solution.py:294
  805.2 82.1 %reduce-scatter.41.cloned.1.call-done = bf16[64,2816]{1,0:T(8,128)(2,1)} async-done(((bf16[1024,2816]{1,0:T(8,128)(2,1)}), bf16[64,2816]{1,0:T(8,128)(2,1)}) %reduce-scatter.41.cloned.1.call-update) | async-done | bytes 360464 | tf_op jit(solution)/shard_map/reduce_scatter | solution.py:291
  903.8 80.5 %reduce-scatter.45.cloned.1.call-done = bf16[176,1024]{1,0:T(8,128)(2,1)} async-done(((bf16[2816,1024]{1,0:T(8,128)(2,1)}), bf16[176,1024]{1,0:T(8,128)(2,1)}) %reduce-scatter.45.cloned.1.call-update) | async-done | bytes 360464 | tf_op jit(solution)/shard_map/reduce_scatter | solution.py:297
  988.5 40.3 %all-reduce.2 = (f32[2,1024]{1,0:T(2,128)S(1)}, f32[3]{0:T(128)S(1)}) all-reduce(f32[2,1024]{1,0:T(2,128)S(1)} %pad_maximum_fusion.2, f32[3]{0:T(128)S(1)} %pad_maximum_fusion.3), channel_id=1, replica_groups=mesh['dp'=2,'seq'=16] {'dp','seq'}, use_global_device_ids=true, to_apply=%region_20.21 | all-reduce | flops 2051 | bytes 16408 | tf_op jit(solution)/shard_map/psum | solution.py:324
  1028.9 20.1 %reduce-scatter.33.cloned.1.call-done = bf16[64,1024]{1,0:T(8,128)(2,1)} async-done(((bf16[1024,1024]{1,0:T(8,128)(2,1)}), bf16[64,1024]{1,0:T(8,128)(2,1)}) %reduce-scatter.33.cloned.1.call-update) | async-done | bytes 131088 | tf_op jit(solution)/shard_map/reduce_scatter | solution.py:285
  1049.6 63.8 %reduce-scatter.29.cloned.1.call-done = bf16[64,1024]{1,0:T(8,128)(2,1)} async-done(((bf16[1024,1024]{1,0:T(8,128)(2,1)}), bf16[64,1024]{1,0:T(8,128)(2,1)}) %reduce-scatter.29.cloned.1.call-update) | async-done | bytes 131088 | tf_op jit(solution)/shard_map/reduce_scatter | solution.py:282
  1114.0 63.8 %reduce-scatter.25.cloned.1.call-done = bf16[64,1024]{1,0:T(8,128)(2,1)} async-done(((bf16[1024,1024]{1,0:T(8,128)(2,1)}), bf16[64,1024]{1,0:T(8,128)(2,1)}) %reduce-scatter.25.cloned.1.call-update) | async-done | bytes 131088 | tf_op jit(solution)/shard_map/reduce_scatter | solution.py:279
  1179.8 15.9 %reduce-scatter.53.cloned.1.call-done = bf16[1408,64]{1,0:T(8,128)(2,1)} async-done(((bf16[2816,64]{1,0:T(8,128)(2,1)}), bf16[1408,64]{1,0:T(8,128)(2,1)}) %reduce-scatter.53.cloned.1.call-update) | async-done | bytes 180240
  1197.6 17.2 %reduce-scatter.51.cloned.1.call-done = bf16[1408,64]{1,0:T(8,128)(2,1)} async-done(((bf16[2816,64]{1,0:T(8,128)(2,1)}), bf16[1408,64]{1,0:T(8,128)(2,1)}) %reduce-scatter.51.cloned.1.call-update) | async-done | bytes 180240
  1216.7 13.2 %reduce-scatter.47.cloned.1.call-done = bf16[176,512]{1,0:T(8,128)(2,1)} async-done(((bf16[176,1024]{1,0:T(8,128)(2,1)}), bf16[176,512]{1,0:T(8,128)(2,1)}) %reduce-scatter.47.cloned.1.call-update) | async-done | bytes 180240 | tf_op jit(solution)/shard_map/reduce_scatter | solution.py:320
  1231.6 10.9 reduce-scatter.35.cloned.1.call-done
  1244.0 11.0 reduce-scatter.31.cloned.1.call-done
  1256.4 11.1 reduce-scatter.27.cloned.1.call-done
  (329 shorter events, 245.8 us)
Async XLA Ops:
  7.2 55.2 %all-gather.10.cloned.1.call-start = ((), (), s32[]{:S(2)}) async-start(), calls=%async_computation.16 | async-start | bytes 2228224 | tf_op jit(solution)/shard_map/all_gather | solution.py:61
  14.9 84.4 %all-gather.14.cloned.1.call-start = ((), (), s32[]{:S(2)}) async-start(), calls=%async_computation.18 | async-start | bytes 2228224 | tf_op jit(solution)/shard_map/all_gather | solution.py:60
  20.3 121.5 %all-gather.18.cloned.1.call-start = ((), (), s32[]{:S(2)}) async-start(), calls=%async_computation.20 | async-start | bytes 2228224 | tf_op jit(solution)/shard_map/all_gather | solution.py:59
  26.5 167.0 %all-gather.12.cloned.1.call-start = ((), (), s32[]{:S(2)}) async-start(), calls=%async_computation.17 | async-start | bytes 4456448 | tf_op jit(solution)/shard_map/all_gather | solution.py:136
  61.2 85.3 %copy-start.23 = (f32[1024]{0:T(1024)}, f32[1024]{0:T(1024)S(1)}, u32[]{:S(2)}) copy-start(f32[1024]{0:T(1024)S(1)} %convert_element_type.252) | copy-start | bytes 12292
  65.3 181.8 %all-gather.16.cloned.1.call-start = ((), (), s32[]{:S(2)}) async-start(), calls=%async_computation.19 | async-start | bytes 4456448 | tf_op jit(solution)/shard_map/all_gather | solution.py:135
  149.9 138.9 %all-gather.20.cloned.1.call-start = ((), (), s32[]{:S(2)}) async-start(), calls=%async_computation.21 | async-start | bytes 2228224 | tf_op jit(solution)/shard_map/all_gather | solution.py:62
  155.0 193.5 %all-gather.24.cloned.1.call-start = ((), (), s32[]{:S(2)}) async-start(), calls=%async_computation.23 | async-start | bytes 6127616 | tf_op jit(solution)/shard_map/all_gather | solution.py:64
  161.4 246.7 %all-gather.22.cloned.1.call-start = ((), (), s32[]{:S(2)}) async-start(), calls=%async_computation.22 | async-start | bytes 6127616 | tf_op jit(solution)/shard_map/all_gather | solution.py:63
  167.8 300.0 %all-gather.26.cloned.1.call-start = ((), (), s32[]{:S(2)}) async-start(), calls=%async_computation.24 | async-start | bytes 6127616 | tf_op jit(solution)/shard_map/all_gather | solution.py:65
  174.1 448.4 %reduce-scatter.37.cloned.1.call-start = ((), (), s32[]{:S(2)}) async-start(), calls=%async_computation.32 | async-start | bytes 2228224 | tf_op jit(solution)/shard_map/reduce_scatter | solution.py:288
  291.8 116.3 %copy-start.4 = (bf16[128,1024]{1,0:T(8,128)(2,1)}, bf16[128,1024]{1,0:T(8,128)(2,1)S(1)}, u32[]{:S(2)}) copy-start(bf16[128,1024]{1,0:T(8,128)(2,1)S(1)} %fusion.113) | copy-start | bytes 786436
  353.1 114.6 %copy-start.19 = (bf16[1,128,1024]{2,1,0:T(8,128)(2,1)S(1)}, bf16[1,128,1024]{2,1,0:T(8,128)(2,1)}, u32[]{:S(2)}) copy-start(bf16[1,128,1024]{2,1,0:T(8,128)(2,1)} %param.23) | copy-start | bytes 786436
  506.7 136.3 %reduce-scatter.23.cloned.1.call-start = ((), (), s32[]{:S(2)}) async-start(), calls=%async_computation.25 | async-start | bytes 4456448 | tf_op jit(solution)/shard_map/reduce_scatter | solution.py:259
  566.1 152.5 %reduce-scatter.49.cloned.1.call-start = ((), (), s32[]{:S(2)}) async-start(), calls=%async_computation.38 | async-start | bytes 4456448
  613.1 189.9 %reduce-scatter.43.cloned.1.call-start = ((), (), s32[]{:S(2)}) async-start(), calls=%async_computation.35 | async-start | bytes 6127616 | tf_op jit(solution)/shard_map/reduce_scatter | solution.py:294
  618.2 269.1 %reduce-scatter.41.cloned.1.call-start = ((), (), s32[]{:S(2)}) async-start(), calls=%async_computation.34 | async-start | bytes 6127616 | tf_op jit(solution)/shard_map/reduce_scatter | solution.py:291
  622.4 276.6 %reduce-scatter.39.cloned.1.call-start = ((), (), s32[]{:S(2)}) async-start(), calls=%async_computation.33 | async-start | bytes 196608 | tf_op jit(solution)/shard_map/reduce_scatter | solution.py:311
  623.0 361.2 %reduce-scatter.45.cloned.1.call-start = ((), (), s32[]{:S(2)}) async-start(), calls=%async_computation.36 | async-start | bytes 6127616 | tf_op jit(solution)/shard_map/reduce_scatter | solution.py:297
  627.8 421.2 %reduce-scatter.33.cloned.1.call-start = ((), (), s32[]{:S(2)}) async-start(), calls=%async_computation.30 | async-start | bytes 2228224 | tf_op jit(solution)/shard_map/reduce_scatter | solution.py:285
  644.0 342.8 %copy-start.16 = (bf16[1,128,1024]{2,1,0:T(8,128)(2,1)}, bf16[1,128,1024]{2,1,0:T(8,128)(2,1)S(1)}, u32[]{:S(2)}) copy-start(bf16[1,128,1024]{2,1,0:T(8,128)(2,1)S(1)} %multiply_convert_fusion.2) | copy-start | bytes 786436
  646.2 467.1 %reduce-scatter.29.cloned.1.call-start = ((), (), s32[]{:S(2)}) async-start(), calls=%async_computation.28 | async-start | bytes 2228224 | tf_op jit(solution)/shard_map/reduce_scatter | solution.py:282
  722.8 455.1 %reduce-scatter.25.cloned.1.call-start = ((), (), s32[]{:S(2)}) async-start(), calls=%async_computation.26 | async-start | bytes 2228224 | tf_op jit(solution)/shard_map/reduce_scatter | solution.py:279
  725.0 470.7 %reduce-scatter.53.cloned.1.call-start = ((), (), s32[]{:S(2)}) async-start(), calls=%async_computation.40 | async-start | bytes 1081344
  805.1 409.6 %reduce-scatter.51.cloned.1.call-start = ((), (), s32[]{:S(2)}) async-start(), calls=%async_computation.39 | async-start | bytes 1081344
  889.5 97.3 %copy-start.6 = (bf16[1024,1024]{1,0:T(8,128)(2,1)S(1)}, bf16[1024,1024]{1,0:T(8,128)(2,1)}, u32[]{:S(2)}) copy-start(bf16[1024,1024]{1,0:T(8,128)(2,1)} %all-gather.10.cloned.1.call-done) | copy-start | bytes 6291460
  889.5 340.4 %reduce-scatter.47.cloned.1.call-start = ((), (), s32[]{:S(2)}) async-start(), calls=%async_computation.37 | async-start | bytes 540672 | tf_op jit(solution)/shard_map/reduce_scatter | solution.py:320
  903.8 145.8 %copy-start.44 = (f32[128]{0:T(128)S(1)}, f32[128]{0:T(128)}, u32[]{:S(2)}) copy-start(f32[128]{0:T(128)} %copy-done.43) | copy-start | bytes 1540
  903.8 274.1 %copy-start.8 = (f32[1,128,1024]{2,1,0:T(8,128)S(1)}, f32[1,128,1024]{2,1,0:T(8,128)}, u32[]{:S(2)}) copy-start(f32[1,128,1024]{2,1,0:T(8,128)} %copy-done.7) | copy-start | bytes 1572868
  984.2 258.2 %reduce-scatter.35.cloned.1.call-start = ((), (), s32[]{:S(2)}) async-start(), calls=%async_computation.31 | async-start | bytes 196608 | tf_op jit(solution)/shard_map/reduce_scatter | solution.py:308
  1049.0 206.0 %reduce-scatter.31.cloned.1.call-start = ((), (), s32[]{:S(2)}) async-start(), calls=%async_computation.29 | async-start | bytes 196608 | tf_op jit(solution)/shard_map/reduce_scatter | solution.py:305
  1113.4 154.2 %reduce-scatter.27.cloned.1.call-start = ((), (), s32[]{:S(2)}) async-start(), calls=%async_computation.27 | async-start | bytes 196608 | tf_op jit(solution)/shard_map/reduce_scatter | solution.py:302
  (50 other events, 995.4 us)
Sparse Core Ops, SparseCore 0:
  15.1 42.0 all-gather.9
  59.3 39.9 all-gather.13
  101.5 40.1 all-gather.17
  144.3 49.0 all-gather.11
  196.0 51.0 all-gather.15
  249.1 39.6 all-gather.19
  291.1 57.3 all-gather.23
  350.7 57.2 all-gather.21
  410.4 57.2 all-gather.25
  506.8 60.4 reduce-scatter.36
  571.2 71.7 reduce-scatter.22
  646.7 71.8 reduce-scatter.48
  722.5 80.4 reduce-scatter.42
  806.7 80.5 reduce-scatter.40
  889.4 9.6 reduce-scatter.38
  902.8 81.3 reduce-scatter.44
  987.8 61.1 reduce-scatter.32
  1052.6 60.7 reduce-scatter.28
  1117.1 60.6 reduce-scatter.24
  1179.9 15.7 reduce-scatter.52
  1197.9 16.7 reduce-scatter.50
  1217.0 12.8 reduce-scatter.46
  1232.1 10.3 reduce-scatter.34
  1244.5 10.3 reduce-scatter.30
  1257.1 10.3 reduce-scatter.26
where the time goes:
time: 1280 us
  waiting for transfers between devices  880 us (69%)
  matrix products  120 us (9%)
  blocking collectives  114 us (9%)
  local copies, waits for them, and re-layouts  111 us (9%)
  other arithmetic  26.5 us (2%)
  between operations  15.6 us (1%)
    unnamed x28, waiting for transfers between devices  106 us
    reduce_scatter x1, waiting for transfers between devices, local(): lax.psum_scatter(grad_gate.astype(jnp.bfloat16), 'seq', scatter_dimension...  82.1 us
    reduce_scatter x1, waiting for transfers between devices, local(): lax.psum_scatter(grad_down.astype(jnp.bfloat16), 'seq', scatter_dimension...  80.5 us
    reduce_scatter x1, waiting for transfers between devices, local(): lax.psum_scatter(grad_up.astype(jnp.bfloat16), 'seq', scatter_dimension=0...  77.9 us
    reduce_scatter x1, waiting for transfers between devices, local(): lax.psum_scatter(grad_query.astype(jnp.bfloat16), 'seq', scatter_dimensio...  63.8 us
    reduce_scatter x1, waiting for transfers between devices, local(): lax.psum_scatter(grad_key.astype(jnp.bfloat16), 'seq', scatter_dimension=...  63.8 us
    unnamed x88, local copies, waits for them, and re-layouts  60.8 us
    all_gather x1, waiting for transfers between devices, fetch_forward(): lax.all_gather(wide_set[5], 'seq', axis=0, tiled=True)  56.7 us
  transfers between devices with their start and end apart: 25, of which 23 were waited for; matrix products, arithmetic and copies ran while one was open for 17% of the time, Pallas kernels for 0%

commit v1 on v0

--- a/solution.py
+++ b/solution.py
@@ -1,3 +1,4 @@
+import functools
 import jax
 import jax.numpy as jnp
 from jax import lax
@@ -6,6 +7,23 @@
 H = 16
 HS = 64
 EPSILON = 1e-06
+
+
+def tell_record_all(load, k_dim):
+    odd, lower = (jax.lax.psum(1, "seq"), jax.lax.axis_index("seq"))
+    frame_out, arr_next = (load, 1)
+    while arr_next < odd:
+        arr_now = jax.lax.ppermute(
+            frame_out, "seq", [(dev_i, dev_i ^ arr_next) for dev_i in range(odd)]
+        )
+        small = jnp.concatenate([frame_out, arr_now], k_dim)
+        back = jnp.concatenate([arr_now, frame_out], k_dim)
+        frame_out = jnp.where(lower & arr_next == 0, small, back)
+        arr_next = 2 * arr_next
+    return frame_out
+
+
+answer_the_types = functools.partial(tell_record_all, k_dim=0)
 
 
 def normalize(rows_in, gain_in):
@@ -60,7 +78,7 @@
         lax.all_gather(wide_set[1], "seq", axis=0, tiled=True),
         lax.all_gather(wide_set[2], "seq", axis=0, tiled=True),
         lax.all_gather(wide_set[3], "seq", axis=0, tiled=True),
-        lax.all_gather(wide_set[4], "seq", axis=0, tiled=True),
+        answer_the_types(wide_set[4]),
         lax.all_gather(wide_set[5], "seq", axis=0, tiled=True),
         lax.all_gather(wide_set[6], "seq", axis=0, tiled=True),
         lax.all_gather(norm1_gain, "seq", axis=0, tiled=True),

time: 1280 us -> 1410 us (1.10)
  waiting for transfers between devices: 880 us -> 976 us
  matrix products: 120 us -> 143 us
    ppermute x0 -> x4, waiting for transfers between devices: none -> 80.2 us  [tell_record_all(): jax.lax.ppermute(frame_out, 'seq', [(dev_i, dev_i ^ arr_next) for dev_i i...]
    all_gather x1, waiting for transfers between devices: 19 us -> 85.6 us  [local(): lax.all_gather(mixed_values, 'seq', axis=1, tiled=True)]
    all_gather x1, waiting for transfers between devices: 54.9 us -> 0.02 us  [fetch_forward(): lax.all_gather(wide_set[6], 'seq', axis=0, tiled=True)]
    reduce_scatter x1, waiting for transfers between devices: 15.2 us -> 69.1 us  [local(): lax.psum_scatter(value_terms.astype(jnp.bfloat16), 'seq', scatter_dimensi...]
    reduce_scatter x1, waiting for transfers between devices: 20.1 us -> 63.8 us  [local(): lax.psum_scatter(grad_value.astype(jnp.bfloat16), 'seq', scatter_dimensio...]
    reduce_scatter x1, waiting for transfers between devices: 63.8 us -> 20.1 us  [local(): lax.psum_scatter(grad_query.astype(jnp.bfloat16), 'seq', scatter_dimensio...]
    unnamed x28, waiting for transfers between devices: 106 us -> 67.2 us
    unnamed x88 -> x80, local copies, waits for them, and re-layouts: 60.8 us -> 60.8 us
  transfers between devices with their start and end apart: 25 -> 29, of which waited for: 23 -> 25; matrix products, arithmetic and copies ran while one was open for 17% -> 18% of each run, Pallas kernels for 0% -> 0%
where the time goes in v1:
time: 1410 us; the launch traced here: 1400 us
  waiting for transfers between devices  976 us (69%)
  matrix products  143 us (10%)
  blocking collectives  114 us (8%)
  local copies, waits for them, and re-layouts  107 us (8%)
  other arithmetic  39.2 us (3%)
  between operations  15.6 us (1%)
    all_gather x1, waiting for transfers between devices, local(): lax.all_gather(mixed_values, 'seq', axis=1, tiled=True)  85.6 us
    reduce_scatter x1, waiting for transfers between devices, local(): lax.psum_scatter(grad_up.astype(jnp.bfloat16), 'seq', scatter_dimension=0...  82.2 us
    reduce_scatter x1, waiting for transfers between devices, local(): lax.psum_scatter(grad_gate.astype(jnp.bfloat16), 'seq', scatter_dimension...  81.1 us
    reduce_scatter x1, waiting for transfers between devices, local(): lax.psum_scatter(grad_down.astype(jnp.bfloat16), 'seq', scatter_dimension...  80.4 us
    ppermute x4, waiting for transfers between devices, tell_record_all(): jax.lax.ppermute(frame_out, 'seq', [(dev_i, dev_i ^ arr_next) for dev_i i...  80.2 us
    reduce_scatter x1, waiting for transfers between devices, local(): lax.psum_scatter(value_terms.astype(jnp.bfloat16), 'seq', scatter_dimensi...  69.1 us
    unnamed x28, waiting for transfers between devices  67.2 us
    reduce_scatter x1, waiting for transfers between devices, local(): lax.psum_scatter(grad_value.astype(jnp.bfloat16), 'seq', scatter_dimensio...  63.8 us
  transfers between devices with their start and end apart: 29, of which 25 were waited for; matrix products, arithmetic and copies ran while one was open for 18% of the time, Pallas kernels for 0%

profile of v1, /device:TPU:0, one launch (start us, length us, event | category | flops | bytes accessed | tf_op | source)
XLA Modules:
  0.0 1402.8 jit_solution(1529408263581037334)
XLA Ops:
  36.7 30.5 %all-reduce.3 = (bf16[1024]{0:T(1024)(128)(2,1)S(1)}, bf16[1024]{0:T(1024)(128)(2,1)S(1)}) all-reduce(bf16[1024]{0:T(1024)(128)(2,1)S(1)} %dynamic-update-slice, bf16[1024]{0:T(1024)(128)(2,1)S(1)} %dynamic-update-slice.1), channel_id=1, replica_groups=mesh['dp'=2,'seq'=16] {'seq'}, use_global_device_ids=true, to_apply=%add | all-reduce | flops 2048 | bytes 8192
  72.4 26.9 %all-gather.18.cloned.1.call-done = bf16[1024,1024]{1,0:T(8,128)(2,1)} async-done(((bf16[64,1024]{1,0:T(8,128)(2,1)}), bf16[1024,1024]{1,0:T(8,128)(2,1)}) %all-gather.18.cloned.1.call-update) | async-done | bytes 2097168 | tf_op jit(solution)/shard_map/all_gather | solution.py:77
  102.2 39.5 %all-gather.14.cloned.1.call-done = bf16[1024,1024]{1,0:T(8,128)(2,1)} async-done(((bf16[64,1024]{1,0:T(8,128)(2,1)}), bf16[1024,1024]{1,0:T(8,128)(2,1)}) %all-gather.14.cloned.1.call-update) | async-done | bytes 2097168 | tf_op jit(solution)/shard_map/all_gather | solution.py:78
  170.5 32.8 %collective-permute-done.1 = bf16[128,2816]{1,0:T(8,128)(2,1)} collective-permute-done((bf16[128,2816]{1,0:T(8,128)(2,1)S(1)}, bf16[128,2816]{1,0:T(8,128)(2,1)}, u32[]{:S(2)}, u32[]{:S(2)}) %collective-permute-start.1) | collective-permute-done | bytes 720928 | tf_op jit(solution)/shard_map/ppermute | solution.py:16
  206.0 45.7 %collective-permute-done.2 = bf16[256,2816]{1,0:T(8,128)(2,1)} collective-permute-done((bf16[256,2816]{1,0:T(8,128)(2,1)S(1)}, bf16[256,2816]{1,0:T(8,128)(2,1)}, u32[]{:S(2)}, u32[]{:S(2)}) %collective-permute-start.2) | collective-permute-done | bytes 1441824 | tf_op jit(solution)/shard_map/ppermute | solution.py:16
  260.9 85.6 %all-gather.12.cloned.1.call-done = bf16[1,2048,1024]{2,1,0:T(8,128)(2,1)} async-done(((bf16[1,128,1024]{2,1,0:T(8,128)(2,1)}), bf16[1,2048,1024]{2,1,0:T(8,128)(2,1)}) %all-gather.12.cloned.1.call-update) | async-done | bytes 4194320 | tf_op jit(solution)/shard_map/all_gather | solution.py:154
  353.0 58.0 %all-gather.16.cloned.1.call-done = bf16[1,2048,1024]{1,2,0:T(8,128)(2,1)} async-done(((bf16[1,128,1024]{1,2,0:T(8,128)(2,1)}), bf16[1,2048,1024]{1,2,0:T(8,128)(2,1)}) %all-gather.16.cloned.1.call-update) | async-done | bytes 4194320 | tf_op jit(solution)/shard_map/all_gather | solution.py:153
  410.9 26.9 %while.50 = (s32[]{:T(128)}, f32[1,16,128]{2,1,0:T(8,128)S(1)}, f32[1,16,128]{2,1,0:T(8,128)S(1)}, s32[2]{0:T(128)S(1)}, s32[1,2048]{1,0:T(1,128)S(1)}, /*index=...) while((s32[]{:T(128)}, f32[1,16,128]{2,1,0:T(8,128)S(1)}, ...), condition=%wide.region_5.6_spmd.clone, body=%wide.region_2.5_spmd.clone.sunk | while | flops 283520128 | bytes 19658448 | solution.py:185
  437.9 14.0 while.51
  457.1 56.7 %all-gather.22.cloned.1.call-done = bf16[1024,2816]{1,0:T(8,128)(2,1)} async-done(((bf16[64,2816]{1,0:T(8,128)(2,1)}), bf16[1024,2816]{1,0:T(8,128)(2,1)}) %all-gather.22.cloned.1.call-update) | async-done | bytes 5767184 | tf_op jit(solution)/shard_map/all_gather | solution.py:82
  526.9 47.1 %all-gather.26.cloned.1.call-done = bf16[1024,2816]{1,0:T(8,128)(2,1)} async-done(((bf16[64,2816]{1,0:T(8,128)(2,1)}), bf16[1024,2816]{1,0:T(8,128)(2,1)}) %all-gather.26.cloned.1.call-update) | async-done | bytes 5767184 | tf_op jit(solution)/shard_map/all_gather | solution.py:104
  586.9 16.0 %while.52 = (s32[]{:T(128)}, f32[1,16,128]{2,1,0:T(8,128)S(1)}, s32[2]{0:T(128)S(1)}, s32[1,2048]{1,0:T(1,128)S(1)}, s32[1,128]{1,0:T(1,128)S(1)}, /*index=5*/bf...) while((s32[]{:T(128)}, f32[1,16,128]{2,1,0:T(8,128)S(1)}, ...), condition=%wide.region_12.13_spmd.clone, body=%wide.region_10.12_spmd.clone.sunk | while | flops 547753088 | bytes 38598400 | solution.py:245
  603.0 48.4 %while.53 = (s32[]{:T(128)}, f32[1,128,16,64]{1,3,2,0:T(8,128)S(1)}, bf16[2,1,1024,16,64]{2,4,3,1,0:T(8,128)(2,1)}, bf16[2,1,1024,16,64]{2,4,3,1,0:T(8,128)(2,1)...) while((s32[]{:T(128)}, ...), condition=%wide.region_14.15_spmd.clone, body=%wide.region_13.14_spmd.clone.sunk | while | flops 1364853888 | bytes 122075984 | solution.py:270
  651.4 11.0 copy.84
  662.4 28.6 %reshape.1048 = bf16[1,2048,1024]{2,0,1:T(2,128)(2,1)} reshape(bf16[2,1,1024,16,64]{4,3,2,0,1:T(8,128)(2,1)} %copy.84) | data formatting | bytes 8388608
  698.1 11.1 copy.77
  709.2 12.1 reshape.1041
  736.7 33.2 %reduce-scatter.49.cloned.1.call-done = bf16[128,1024]{1,0:T(8,128)(2,1)} async-done(((bf16[2048,1024]{1,0:T(8,128)(2,1)}), bf16[128,1024]{1,0:T(8,128)(2,1)}) %reduce-scatter.49.cloned.1.call-update) | async-done | bytes 262160
  776.4 69.1 %reduce-scatter.23.cloned.1.call-done = bf16[1,128,1024]{2,1,0:T(8,128)(2,1)} async-done(((bf16[1,2048,1024]{2,1,0:T(8,128)(2,1)}), bf16[1,128,1024]{2,1,0:T(8,128)(2,1)}) %reduce-scatter.23.cloned.1.call-update) | async-done | bytes 262160 | tf_op jit(solution)/shard_map/reduce_scatter | solution.py:277
  848.7 81.1 %reduce-scatter.41.cloned.1.call-done = bf16[64,2816]{1,0:T(8,128)(2,1)} async-done(((bf16[1024,2816]{1,0:T(8,128)(2,1)}), bf16[64,2816]{1,0:T(8,128)(2,1)}) %reduce-scatter.41.cloned.1.call-update) | async-done | bytes 360464 | tf_op jit(solution)/shard_map/reduce_scatter | solution.py:309
  932.0 82.2 %reduce-scatter.43.cloned.1.call-done = bf16[64,2816]{1,0:T(8,128)(2,1)} async-done(((bf16[1024,2816]{1,0:T(8,128)(2,1)}), bf16[64,2816]{1,0:T(8,128)(2,1)}) %reduce-scatter.43.cloned.1.call-update) | async-done | bytes 360464 | tf_op jit(solution)/shard_map/reduce_scatter | solution.py:312
  1030.7 80.4 %reduce-scatter.45.cloned.1.call-done = bf16[176,1024]{1,0:T(8,128)(2,1)} async-done(((bf16[2816,1024]{1,0:T(8,128)(2,1)}), bf16[176,1024]{1,0:T(8,128)(2,1)}) %reduce-scatter.45.cloned.1.call-update) | async-done | bytes 360464 | tf_op jit(solution)/shard_map/reduce_scatter | solution.py:315
  1115.5 40.3 %all-reduce.2 = (f32[2,1024]{1,0:T(2,128)S(1)}, f32[3]{0:T(128)S(1)}) all-reduce(f32[2,1024]{1,0:T(2,128)S(1)} %pad_maximum_fusion.2, f32[3]{0:T(128)S(1)} %pad_maximum_fusion.3), channel_id=1, replica_groups=mesh['dp'=2,'seq'=16] {'dp','seq'}, use_global_device_ids=true, to_apply=%region_20.21 | all-reduce | flops 2051 | bytes 16408 | tf_op jit(solution)/shard_map/psum | solution.py:342
  1155.8 20.1 %reduce-scatter.25.cloned.1.call-done = bf16[64,1024]{1,0:T(8,128)(2,1)} async-done(((bf16[1024,1024]{1,0:T(8,128)(2,1)}), bf16[64,1024]{1,0:T(8,128)(2,1)}) %reduce-scatter.25.cloned.1.call-update) | async-done | bytes 131088 | tf_op jit(solution)/shard_map/reduce_scatter | solution.py:297
  1176.6 63.8 %reduce-scatter.29.cloned.1.call-done = bf16[64,1024]{1,0:T(8,128)(2,1)} async-done(((bf16[1024,1024]{1,0:T(8,128)(2,1)}), bf16[64,1024]{1,0:T(8,128)(2,1)}) %reduce-scatter.29.cloned.1.call-update) | async-done | bytes 131088 | tf_op jit(solution)/shard_map/reduce_scatter | solution.py:300
  1241.0 63.8 %reduce-scatter.33.cloned.1.call-done = bf16[64,1024]{1,0:T(8,128)(2,1)} async-done(((bf16[1024,1024]{1,0:T(8,128)(2,1)}), bf16[64,1024]{1,0:T(8,128)(2,1)}) %reduce-scatter.33.cloned.1.call-update) | async-done | bytes 131088 | tf_op jit(solution)/shard_map/reduce_scatter | solution.py:303
  1306.8 15.9 %reduce-scatter.51.cloned.1.call-done = bf16[1408,64]{1,0:T(8,128)(2,1)} async-done(((bf16[2816,64]{1,0:T(8,128)(2,1)}), bf16[1408,64]{1,0:T(8,128)(2,1)}) %reduce-scatter.51.cloned.1.call-update) | async-done | bytes 180240
  1324.6 17.2 %reduce-scatter.53.cloned.1.call-done = bf16[1408,64]{1,0:T(8,128)(2,1)} async-done(((bf16[2816,64]{1,0:T(8,128)(2,1)}), bf16[1408,64]{1,0:T(8,128)(2,1)}) %reduce-scatter.53.cloned.1.call-update) | async-done | bytes 180240
  1343.7 13.2 reduce-scatter.47.cloned.1.call-done
  1358.6 10.9 reduce-scatter.27.cloned.1.call-done
  1371.0 11.0 reduce-scatter.31.cloned.1.call-done
  1383.5 11.1 reduce-scatter.35.cloned.1.call-done
  (309 shorter events, 282.1 us)
Async XLA Ops:
  7.2 61.2 %all-gather.10.cloned.1.call-start = ((), (), s32[]{:S(2)}) async-start(), calls=%async_computation.16 | async-start | bytes 2228224 | tf_op jit(solution)/shard_map/all_gather | solution.py:79
  14.9 84.3 %all-gather.18.cloned.1.call-start = ((), (), s32[]{:S(2)}) async-start(), calls=%async_computation.20 | async-start | bytes 2228224 | tf_op jit(solution)/shard_map/all_gather | solution.py:77
  20.3 121.4 %all-gather.14.cloned.1.call-start = ((), (), s32[]{:S(2)}) async-start(), calls=%async_computation.18 | async-start | bytes 2228224 | tf_op jit(solution)/shard_map/all_gather | solution.py:78
  26.5 228.7 %all-gather.24.cloned.1.call-start = ((), (), s32[]{:S(2)}) async-start(), calls=%async_computation.23 | async-start | bytes 6127616 | tf_op jit(solution)/shard_map/all_gather | solution.py:83
  33.1 313.4 %all-gather.12.cloned.1.call-start = ((), (), s32[]{:S(2)}) async-start(), calls=%async_computation.17 | async-start | bytes 4456448 | tf_op jit(solution)/shard_map/all_gather | solution.py:154
  71.3 339.6 %all-gather.16.cloned.1.call-start = ((), (), s32[]{:S(2)}) async-start(), calls=%async_computation.19 | async-start | bytes 4456448 | tf_op jit(solution)/shard_map/all_gather | solution.py:153
  149.8 304.3 %all-gather.20.cloned.1.call-start = ((), (), s32[]{:S(2)}) async-start(), calls=%async_computation.21 | async-start | bytes 2228224 | tf_op jit(solution)/shard_map/all_gather | solution.py:80
  154.9 358.9 %all-gather.22.cloned.1.call-start = ((), (), s32[]{:S(2)}) async-start(), calls=%async_computation.22 | async-start | bytes 6127616 | tf_op jit(solution)/shard_map/all_gather | solution.py:82
  161.6 412.5 %all-gather.26.cloned.1.call-start = ((), (), s32[]{:S(2)}) async-start(), calls=%async_computation.24 | async-start | bytes 6127616 | tf_op jit(solution)/shard_map/all_gather | solution.py:104
  167.8 1.7 collective-permute-start
  169.6 33.6 %collective-permute-start.1 = (bf16[128,2816]{1,0:T(8,128)(2,1)S(1)}, bf16[128,2816]{1,0:T(8,128)(2,1)}, u32[]{:S(2)}, u32[]{:S(2)}) collective-permute-start(bf16[128,2816]{1,0:T(8,128)(2,1)S(1)} %maximum_select_fusion.4), channel_id=1, source_target_pairs={{0,2},{1,3},{2,0},{3,1},{4,6},{5,7},{6,4},{7,5},{8,10},{9,11},{10,... | collective-permute-start | bytes 2162696 | tf_op jit(solution)/shard_map/ppermute | solution.py:16
  205.5 46.2 %collective-permute-start.2 = (bf16[256,2816]{1,0:T(8,128)(2,1)S(1)}, bf16[256,2816]{1,0:T(8,128)(2,1)}, u32[]{:S(2)}, u32[]{:S(2)}) collective-permute-start(bf16[256,2816]{1,0:T(8,128)(2,1)S(1)} %maximum_select_fusion.3), channel_id=1, source_target_pairs={{0,4},{1,5},{2,6},{3,7},{4,0},{5,1},{6,2},{7,3},{8,12},{9,13},{10,... | collective-permute-start | bytes 4325384 | tf_op jit(solution)/shard_map/ppermute | solution.py:16
  205.6 525.6 %reduce-scatter.37.cloned.1.call-start = ((), (), s32[]{:S(2)}) async-start(), calls=%async_computation.32 | async-start | bytes 2228224 | tf_op jit(solution)/shard_map/reduce_scatter | solution.py:306
  255.1 262.5 %collective-permute-start.3 = (bf16[512,2816]{1,0:T(8,128)(2,1)}, bf16[512,2816]{1,0:T(8,128)(2,1)}, u32[]{:S(2)}, u32[]{:S(2)}) collective-permute-start(bf16[512,2816]{1,0:T(8,128)(2,1)} %maximum_select_fusion.2), channel_id=1, source_target_pairs={{0,8},{1,9},{2,10},{3,11},{4,12},{5,13},{6,14},{7,15},{8,0},{9,1},... | collective-permute-start | bytes 8650760 | tf_op jit(solution)/shard_map/ppermute | solution.py:16
  602.9 166.9 %reduce-scatter.49.cloned.1.call-start = ((), (), s32[]{:S(2)}) async-start(), calls=%async_computation.38 | async-start | bytes 4456448
  698.1 147.4 %reduce-scatter.23.cloned.1.call-start = ((), (), s32[]{:S(2)}) async-start(), calls=%async_computation.25 | async-start | bytes 4456448 | tf_op jit(solution)/shard_map/reduce_scatter | solution.py:277
  721.3 208.5 %reduce-scatter.41.cloned.1.call-start = ((), (), s32[]{:S(2)}) async-start(), calls=%async_computation.34 | async-start | bytes 6127616 | tf_op jit(solution)/shard_map/reduce_scatter | solution.py:309
  725.7 288.6 %reduce-scatter.43.cloned.1.call-start = ((), (), s32[]{:S(2)}) async-start(), calls=%async_computation.35 | async-start | bytes 6127616 | tf_op jit(solution)/shard_map/reduce_scatter | solution.py:312
  731.2 294.8 %reduce-scatter.39.cloned.1.call-start = ((), (), s32[]{:S(2)}) async-start(), calls=%async_computation.33 | async-start | bytes 196608 | tf_op jit(solution)/shard_map/reduce_scatter | solution.py:329
  731.8 379.4 %reduce-scatter.45.cloned.1.call-start = ((), (), s32[]{:S(2)}) async-start(), calls=%async_computation.36 | async-start | bytes 6127616 | tf_op jit(solution)/shard_map/reduce_scatter | solution.py:315
  736.6 439.3 %reduce-scatter.25.cloned.1.call-start = ((), (), s32[]{:S(2)}) async-start(), calls=%async_computation.26 | async-start | bytes 2228224 | tf_op jit(solution)/shard_map/reduce_scatter | solution.py:297
  774.1 466.2 %reduce-scatter.29.cloned.1.call-start = ((), (), s32[]{:S(2)}) async-start(), calls=%async_computation.28 | async-start | bytes 2228224 | tf_op jit(solution)/shard_map/reduce_scatter | solution.py:300
  776.3 528.5 %reduce-scatter.33.cloned.1.call-start = ((), (), s32[]{:S(2)}) async-start(), calls=%async_computation.30 | async-start | bytes 2228224 | tf_op jit(solution)/shard_map/reduce_scatter | solution.py:303
  846.5 267.3 %copy-start.18 = (bf16[1,128,1024]{2,1,0:T(8,128)(2,1)}, bf16[1,128,1024]{2,1,0:T(8,128)(2,1)S(1)}, u32[]{:S(2)}) copy-start(bf16[1,128,1024]{2,1,0:T(8,128)(2,1)S(1)} %multiply_convert_fusion.2) | copy-start | bytes 786436
  848.6 474.0 %reduce-scatter.51.cloned.1.call-start = ((), (), s32[]{:S(2)}) async-start(), calls=%async_computation.39 | async-start | bytes 1081344
  932.0 409.8 %reduce-scatter.53.cloned.1.call-start = ((), (), s32[]{:S(2)}) async-start(), calls=%async_computation.40 | async-start | bytes 1081344
  1016.4 340.5 %reduce-scatter.47.cloned.1.call-start = ((), (), s32[]{:S(2)}) async-start(), calls=%async_computation.37 | async-start | bytes 540672 | tf_op jit(solution)/shard_map/reduce_scatter | solution.py:338
  1030.7 145.8 %copy-start.34 = (f32[128]{0:T(128)S(1)}, f32[128]{0:T(128)}, u32[]{:S(2)}) copy-start(f32[128]{0:T(128)} %copy-done.33) | copy-start | bytes 1540
  1030.7 274.1 %copy-start.7 = (f32[1,128,1024]{2,1,0:T(8,128)S(1)}, f32[1,128,1024]{2,1,0:T(8,128)}, u32[]{:S(2)}) copy-start(f32[1,128,1024]{2,1,0:T(8,128)} %copy-done.6) | copy-start | bytes 1572868
  1111.2 258.3 %reduce-scatter.27.cloned.1.call-start = ((), (), s32[]{:S(2)}) async-start(), calls=%async_computation.27 | async-start | bytes 196608 | tf_op jit(solution)/shard_map/reduce_scatter | solution.py:320
  1176.0 206.0 %reduce-scatter.31.cloned.1.call-start = ((), (), s32[]{:S(2)}) async-start(), calls=%async_computation.29 | async-start | bytes 196608 | tf_op jit(solution)/shard_map/reduce_scatter | solution.py:323
  1240.3 154.2 %reduce-scatter.35.cloned.1.call-start = ((), (), s32[]{:S(2)}) async-start(), calls=%async_computation.31 | async-start | bytes 196608 | tf_op jit(solution)/shard_map/reduce_scatter | solution.py:326
  (38 other events, 1024.6 us)
Sparse Core Ops, SparseCore 0:
  15.1 41.9 all-gather.9
  59.2 40.0 all-gather.17
  101.4 40.1 all-gather.13
  143.8 75.3 all-gather.23
  221.8 124.6 all-gather.11
  349.1 61.7 all-gather.15
  413.1 40.9 all-gather.19
  456.3 57.4 all-gather.21
  516.7 57.2 all-gather.25
  603.1 60.4 reduce-scatter.36
  698.2 71.6 reduce-scatter.48
  773.6 71.8 reduce-scatter.22
  849.4 80.4 reduce-scatter.40
  933.6 80.6 reduce-scatter.42
  1016.3 9.6 reduce-scatter.38
  1029.7 81.3 reduce-scatter.44
  1114.8 61.1 reduce-scatter.24
  1179.5 60.7 reduce-scatter.28
  1244.0 60.7 reduce-scatter.32
  1306.9 15.7 reduce-scatter.50
  1324.9 16.7 reduce-scatter.52
  1344.0 12.8 reduce-scatter.46
  1359.1 10.3 reduce-scatter.26
  1371.6 10.3 reduce-scatter.30
  1384.2 10.3 reduce-scatter.34
